TPU v7x, 256 devices: a whole 4x4x8 slice. The times are simulated.
256 devices in a mesh: samp: 64 (over z, y, core), var: 4 (over x).
Axes of the slice: x: 4, y: 4, z: 8, core: 2. Of those that a mesh axis runs over, the one named last changes fastest.
Arguments:
- dosage: bfloat16 [16384, 40960], P('samp', 'var'), may hold values from 0 to 2
- centers: float32 [40960], replicated, may hold values from 0.4 to 1.34
- scales: float32 [40960], replicated, may hold values from 1.6 to 2.2
- phenotype: float32 [16384], P('samp'), may hold values from -6 to 6
- fold_ids: int32 [16384], P('samp'), may hold values from 0 to 3
- strong_blocks: int32 [32], replicated, may hold values from 0 to 319, as said below
- warm_start: float32 [4096, 32], replicated, may hold values from -4 to 4
- penalty: float32 [8], replicated, may hold values from 0.05 to 0.5
- step_size: float32 [32], replicated, may hold values from 0.2 to 0.6
Outputs:
- margin: float32 [40960], P('var')
- coefficients: float32 [4096, 32], P('var')
Inputs may be any that keep to these rules, and one draw needn't show every extreme that they name: `strong_blocks`: 32 different block numbers.
All inputs are finite; a program needn't handle non-finite values.
Results may differ from a plain program's by a relative error of at most 0.0075.
Values may be sent and summed in bfloat16 or wider, within the bound.
No kernel may reach another device: no remote copies, remote signals or barrier semaphores. Data moves between devices by JAX's collectives and lax.ppermute only.
A program may use at most 64 MiB of HBM per device.

v0:
```python
import math
import jax
import jax.numpy as jnp
from jax import lax
from jax.sharding import PartitionSpec as P

BLOCK = 128
NS = 4096
LAMBDAS = 8
FOLDS = 4
ITERS = 3
exact_mode = lax.Precision.HIGHEST


def shards(
    dosage, centers, scales, phenotype, fold_ids, strong_blocks, warm_start, penalty, step_size
):
    rows, local_width = dosage.shape
    groups = lax.axis_size("var")
    place = lax.axis_index("var")
    fit_total = LAMBDAS * FOLDS
    fit_folds = jnp.arange(fit_total, dtype=jnp.int32) % FOLDS
    weights = (fold_ids[:, None] != fit_folds[None, :]).astype(jnp.float32)
    counts = lax.psum(jnp.sum(weights, axis=0), "samp")
    fit_penalty = jnp.repeat(penalty, FOLDS)
    threshold = step_size * fit_penalty
    local_blocks = local_width // BLOCK
    relative = strong_blocks - place * local_blocks
    owned = (relative >= 0) & (relative < local_blocks)
    picked = jnp.take(
        dosage.reshape(rows, local_blocks, BLOCK), jnp.clip(relative, 0, local_blocks - 1), axis=1
    )
    masked = (picked * owned.astype(jnp.bfloat16)[None, :, None]).reshape(rows, NS)
    columns = (
        strong_blocks[:, None] * BLOCK + jnp.arange(BLOCK, dtype=jnp.int32)[None, :]
    ).reshape(NS)
    strong_centers = centers[columns]
    strong_scales = scales[columns]
    owned_columns = jnp.repeat(owned.astype(jnp.float32), BLOCK)
    share = NS // groups
    point = warm_start
    part_centers = strong_centers * owned_columns
    part_threshold = threshold[None, :]

    def residual_of(coef):
        scaled = (strong_scales[:, None] * coef).astype(jnp.bfloat16)
        partial_fit = jnp.dot(masked, scaled, preferred_element_type=jnp.float32)
        partial_fit = (
            partial_fit - jnp.dot(part_centers * strong_scales, coef, precision=exact_mode)[None, :]
        )
        fitted = lax.psum(partial_fit.astype(jnp.bfloat16), "var").astype(jnp.float32)
        return (weights * (phenotype[:, None] - fitted)).astype(jnp.bfloat16)

    rounded = residual_of(point)
    column_sums = jnp.sum(rounded.astype(jnp.float32), axis=0)
    local_centers = lax.dynamic_slice_in_dim(centers, place * local_width, local_width, 0)
    local_scales = lax.dynamic_slice_in_dim(scales, place * local_width, local_width, 0)
    cross = lax.dot_general(
        dosage, rounded, (((0,), (0,)), ((), ())), preferred_element_type=jnp.float32
    )
    total = lax.psum(cross - local_centers[:, None] * column_sums[None, :], "samp")
    margin = jnp.max(
        jnp.abs(local_scales[:, None] * total / counts[None, :]) / fit_penalty[None, :], axis=1
    )
    momentum = 1.0
    previous = point
    for sweep in range(ITERS):
        if sweep > 0:
            rounded = residual_of(point)
            column_sums = jnp.sum(rounded.astype(jnp.float32), axis=0)
        gradient_cross = lax.dot_general(
            masked, rounded, (((0,), (0,)), ((), ())), preferred_element_type=jnp.float32
        )
        gradient_cross = gradient_cross - part_centers[:, None] * column_sums[None, :]
        gradient_total = lax.psum(gradient_cross, ("samp", "var"))
        moved = point + step_size[None, :] * (
            strong_scales[:, None] * gradient_total / counts[None, :]
        )
        current = moved - jnp.clip(moved, -part_threshold, part_threshold)
        following = (1.0 + math.sqrt(1.0 + 4.0 * momentum * momentum)) / 2.0
        point = current + (momentum - 1.0) / following * (current - previous)
        previous = current
        momentum = following
    coefficients = lax.dynamic_slice_in_dim(previous, place * share, share, 0)
    return (margin, coefficients)


def solution(mesh):
    return jax.shard_map(
        shards,
        mesh=mesh,
        in_specs=(P("samp", "var"), P(), P(), P("samp"), P("samp"), P(), P(), P(), P()),
        out_specs=(P("var"), P("var", None)),
        check_vma=False,
    )
```

profile of v0, /device:TPU:2, one launch (start us, length us, event | category | flops | bytes accessed | tf_op | source)
XLA Modules:
  0.0 1087.9 jit_solution(17105678928884932665)
XLA Ops:
  7.2 7.9 copy.11
  15.2 7.9 copy.12
  23.1 3.4 gather_fusion
  26.6 2.9 copy.13
  29.8 23.0 %gather_fusion.1 = f32[4096]{0:T(1024)S(1)} fusion(f32[40960]{0:T(1024)S(1)} %copy-done.1, s32[4096]{0:T(1024)S(1)} %broadcast_clamp_fusion), kind=kCustom, calls=%fused_computation.1 | custom fusion | bytes 49152 | tf_op jit(solution)/shard_map/gather | solution.py:38
  52.9 23.0 %gather_fusion.2 = f32[4096]{0:T(1024)S(1)} fusion(f32[40960]{0:T(1024)S(1)} %copy-done, s32[4096]{0:T(1024)S(1)} %broadcast_clamp_fusion), kind=kCustom, calls=%fused_computation.2 | custom fusion | bytes 49152 | tf_op jit(solution)/shard_map/gather | solution.py:37
  76.0 0.5 convolution_bitcast_fusion.3
  76.5 3.2 fusion.1
  79.7 0.4 fusion.3
  80.2 15.3 %psum.56 = bf16[256,32]{0,1:T(8,128)(2,1)S(1)} all-reduce(bf16[256,32]{0,1:T(8,128)(2,1)S(1)} %fusion.3), channel_id=1, replica_groups=mesh['samp'=64,'var'=4] {'var'}, use_global_device_ids=true, to_apply=%region_0.1 | all-reduce | flops 8192 | bytes 32768 | tf_op jit(solution)/shard_map/psum | solution.py:51
  95.5 0.2 fusion.11
  95.7 1.5 convolution_subtract_fusion.2
  97.4 127.1 %psum.58 = f32[32]{0:T(128)S(1)} all-reduce(f32[32]{0:T(128)S(1)} %get-tuple-element.2), channel_id=1, replica_groups=mesh['samp'=64,'var'=4] {'samp'}, use_global_device_ids=true, to_apply=%region_4.5 | all-reduce | flops 32 | bytes 256 | tf_op jit(solution)/shard_map/psum | solution.py:24
  224.5 131.6 %all-reduce.7.cloned.1.call-done = f32[4096,32]{0,1:T(8,128)} async-done(((f32[4096,32]{0,1:T(8,128)}), f32[4096,32]{0,1:T(8,128)}) %all-reduce.7.cloned.1.call-update) | async-done | bytes 524304 | tf_op jit(solution)/shard_map/psum | solution.py:75
  356.1 1.8 convolution_bitcast_fusion.2
  357.9 0.5 fusion.4
  358.5 14.0 %psum.60 = bf16[256,32]{0,1:T(8,128)(2,1)S(1)} all-reduce(bf16[256,32]{0,1:T(8,128)(2,1)S(1)} %fusion.4), channel_id=1, replica_groups=mesh['samp'=64,'var'=4] {'var'}, use_global_device_ids=true, to_apply=%region_7.8 | all-reduce | flops 8192 | bytes 32768 | tf_op jit(solution)/shard_map/psum | solution.py:51
  372.5 0.2 convert_reduce_fusion.1
  372.7 1.5 convolution_subtract_fusion.1
  374.3 4.6 fusion
  379.0 250.2 %all-reduce.9.cloned.1.call-done = f32[4096,32]{0,1:T(8,128)} async-done(((f32[4096,32]{0,1:T(8,128)}), f32[4096,32]{0,1:T(8,128)}) %all-reduce.9.cloned.1.call-update) | async-done | bytes 524304 | tf_op jit(solution)/shard_map/psum | solution.py:75
  629.3 1.6 multiply_add_fusion
  630.9 0.5 convolution_bitcast_fusion.1
  631.4 0.4 fusion.5
  631.9 13.9 %psum.62 = bf16[256,32]{0,1:T(8,128)(2,1)S(1)} all-reduce(bf16[256,32]{0,1:T(8,128)(2,1)S(1)} %fusion.5), channel_id=1, replica_groups=mesh['samp'=64,'var'=4] {'var'}, use_global_device_ids=true, to_apply=%region_10.11 | all-reduce | flops 8192 | bytes 32768 | tf_op jit(solution)/shard_map/psum | solution.py:51
  645.8 0.2 convert_reduce_fusion
  646.0 1.5 convolution_subtract_fusion
  647.5 172.9 %all-reduce.5.cloned.1.call-done = f32[10240,32]{0,1:T(8,128)} async-done(((f32[10240,32]{0,1:T(8,128)}), f32[10240,32]{0,1:T(8,128)}) %all-reduce.5.cloned.1.call-update) | async-done | bytes 1310736 | tf_op jit(solution)/shard_map/psum | solution.py:61
  820.4 2.3 fusion.2
  822.7 256.9 %all-reduce.11.cloned.1.call-done = f32[4096,32]{0,1:T(8,128)} async-done(((f32[4096,32]{0,1:T(8,128)}), f32[4096,32]{0,1:T(8,128)}) %all-reduce.11.cloned.1.call-update) | async-done | bytes 524304 | tf_op jit(solution)/shard_map/psum | solution.py:75
  1079.6 1.1 broadcast_multiply_fusion
  1080.6 0.8 minimum_subtract_fusion.1
  (48 shorter events, 0.8 us)
Async XLA Ops:
  7.2 348.9 %all-reduce.7.cloned.1.call-start = ((), (), s32[]{:S(2)}) async-start(), calls=%async_computation.1 | async-start | bytes 1048576 | tf_op jit(solution)/shard_map/psum | solution.py:75
  15.2 7.9 copy-start.10
  26.6 3.2 copy-start.1
  29.8 23.1 %copy-start = (f32[40960]{0:T(1024)S(1)}, f32[40960]{0:T(1024)}, u32[]{:S(2)}) copy-start(f32[40960]{0:T(1024)} %param.10) | copy-start | bytes 491524
  52.8 23.1 %copy-start.2 = (f32[4096,32]{0,1:T(8,128)S(1)}, f32[4096,32]{0,1:T(8,128)}, u32[]{:S(2)}) copy-start(f32[4096,32]{0,1:T(8,128)} %param.15) | copy-start | bytes 1572868
  79.7 15.8 %copy-start.4 = (s32[256]{0:T(256)S(1)}, s32[256]{0:T(256)}, u32[]{:S(2)}) copy-start(s32[256]{0:T(256)} %param.13) | copy-start | bytes 3076
  79.7 15.8 %copy-start.5 = (f32[256]{0:T(256)S(1)}, f32[256]{0:T(256)}, u32[]{:S(2)}) copy-start(f32[256]{0:T(256)} %param.12) | copy-start | bytes 3076
  80.1 17.1 %copy-start.9 = (f32[8]{0:T(128)S(1)}, f32[8]{0:T(128)}, u32[]{:S(2)}) copy-start(f32[8]{0:T(128)} %param.16) | copy-start | bytes 100
  80.2 144.4 %copy-start.6 = (f32[32]{0:T(128)S(1)}, f32[32]{0:T(128)}, u32[]{:S(2)}) copy-start(f32[32]{0:T(128)} %param.17) | copy-start | bytes 388
  95.7 128.9 %copy-start.7 = (f32[32]{0:T(128)}, f32[32]{0:T(128)S(1)}, u32[]{:S(2)}) copy-start(f32[32]{0:T(128)S(1)} %get-tuple-element.3) | copy-start | bytes 388
  97.2 532.1 %all-reduce.9.cloned.1.call-start = ((), (), s32[]{:S(2)}) async-start(), calls=%async_computation.2 | async-start | bytes 1048576 | tf_op jit(solution)/shard_map/psum | solution.py:75
  356.1 1.8 copy-start.3
  358.5 15.9 %dynamic-slice-start = ((f32[40960]{0:T(1024)}, s32[]{:T(128)}), f32[10240]{0:T(1024)S(1)}, s32[]{:S(2)}) async-start(f32[40960]{0:T(1024)} %param.10, s32[]{:T(128)} %select_n.39), calls=%async_computation.4 | async-start | bytes 82432 | tf_op jit(solution)/shard_map/dynamic_slice | solution.py:56
  358.5 15.9 %copy-start.8 = (f32[32]{0:T(128)S(1)}, f32[32]{0:T(128)}, u32[]{:S(2)}) copy-start(f32[32]{0:T(128)} %copy-done.7) | copy-start | bytes 388
  374.3 446.2 %all-reduce.5.cloned.1.call-start = ((), (), s32[]{:S(2)}) async-start(), calls=%async_computation | async-start | bytes 2621440 | tf_op jit(solution)/shard_map/psum | solution.py:61
  379.0 700.6 %all-reduce.11.cloned.1.call-start = ((), (), s32[]{:S(2)}) async-start(), calls=%async_computation.3 | async-start | bytes 1048576 | tf_op jit(solution)/shard_map/psum | solution.py:75
  631.9 188.6 %dynamic-slice-start.1 = ((f32[40960]{0:T(1024)}, s32[]{:T(128)}), f32[10240]{0:T(1024)S(1)}, s32[]{:S(2)}) async-start(f32[40960]{0:T(1024)} %param.11, s32[]{:T(128)} %select_n.39), calls=%async_computation.5 | async-start | bytes 82432 | tf_op jit(solution)/shard_map/dynamic_slice | solution.py:57
Sparse Core Ops, SparseCore 0:
  97.3 258.7 all-reduce.6
  374.4 254.8 all-reduce.8
  632.7 187.6 all-reduce.4
  825.7 253.7 all-reduce.10
where the time goes:
time: 1090 us
  waiting for transfers between devices  812 us (74%)
  blocking collectives  170 us (16%)
  local copies, waits for them, and re-layouts  68.7 us (6%)
  between operations  14 us (1%)
  matrix products  13.4 us (1%)
    psum x3, waiting for transfers between devices, shards(): gradient_total = lax.psum(gradient_cross, ('samp', 'var'))  639 us
    psum x1, waiting for transfers between devices, shards(): lax.psum(cross - local_centers[:, None] * column_sums[None, :], 'samp')  173 us
    psum x1, blocking collectives, shards(): counts = lax.psum(jnp.sum(weights, axis=0), 'samp')  127 us
    psum x3, blocking collectives, residual_of(): lax.psum(partial_fit.astype(jnp.bfloat16), 'var').astype(jnp.float32)  43.3 us
    gather x1, local copies, waits for them, and re-layouts, shards(): strong_scales = scales[columns]  23 us
    gather x1, local copies, waits for them, and re-layouts, shards(): strong_centers = centers[columns]  23 us
  transfers between devices with their start and end apart: 4, of which 4 were waited for; matrix products, arithmetic and copies ran while one was open for 1% of the time, Pallas kernels for 0%

commit v1 on v0

--- a/solution.py
+++ b/solution.py
@@ -72,7 +72,13 @@
             masked, rounded, (((0,), (0,)), ((), ())), preferred_element_type=jnp.float32
         )
         gradient_cross = gradient_cross - part_centers[:, None] * column_sums[None, :]
-        gradient_total = lax.psum(gradient_cross, ("samp", "var"))
+
+        def _link_flows(z_in):
+            for k0 in ("var", "samp"):
+                z_in = lax.psum(z_in, k0)
+            return z_in
+
+        gradient_total = _link_flows(gradient_cross)
         moved = point + step_size[None, :] * (
             strong_scales[:, None] * gradient_total / counts[None, :]
         )

time: 1090 us -> 859 us (0.79)
  waiting for transfers between devices: 812 us -> 580 us
    psum x3 -> x5, waiting for transfers between devices: 639 us -> 385 us  [_link_flows(): z_in = lax.psum(z_in, k0)]
    psum x1, waiting for transfers between devices: 173 us -> 195 us  [shards(): lax.psum(cross - local_centers[:, None] * column_sums[None, :], 'samp')]
  transfers between devices with their start and end apart: 4 -> 6, of which waited for: 4 -> 6; matrix products, arithmetic and copies ran while one was open for 1% -> 1% of each run, Pallas kernels for 0% -> 0%
where the time goes in v1:
time: 859 us
  waiting for transfers between devices  580 us (68%)
  blocking collectives  171 us (20%)
  local copies, waits for them, and re-layouts  68.7 us (8%)
  matrix products  14.6 us (2%)
  between operations  14.4 us (2%)
  other arithmetic  10.3 us (1%)
    psum x5, waiting for transfers between devices, _link_flows(): z_in = lax.psum(z_in, k0)  385 us
    psum x1, waiting for transfers between devices, shards(): lax.psum(cross - local_centers[:, None] * column_sums[None, :], 'samp')  195 us
    psum x1, blocking collectives, shards(): counts = lax.psum(jnp.sum(weights, axis=0), 'samp')  127 us
    psum x3, blocking collectives, residual_of(): lax.psum(partial_fit.astype(jnp.bfloat16), 'var').astype(jnp.float32)  43.8 us
    gather x1, local copies, waits for them, and re-layouts, shards(): strong_scales = scales[columns]  23 us
    gather x1, local copies, waits for them, and re-layouts, shards(): strong_centers = centers[columns]  23 us
  transfers between devices with their start and end apart: 6, of which 6 were waited for; matrix products, arithmetic and copies ran while one was open for 1% of the time, Pallas kernels for 0%

profile of v1, /device:TPU:2, one launch (start us, length us, event | category | flops | bytes accessed | tf_op | source)
XLA Modules:
  0.0 858.6 jit_solution(11217240243256080008)
XLA Ops:
  7.2 7.9 copy.11
  15.2 7.9 copy.12
  23.1 3.4 gather_fusion
  26.6 2.9 copy.13
  29.8 23.0 %gather_fusion.1 = f32[4096]{0:T(1024)S(1)} fusion(f32[40960]{0:T(1024)S(1)} %copy-done.1, s32[4096]{0:T(1024)S(1)} %broadcast_clamp_fusion), kind=kCustom, calls=%fused_computation.1 | custom fusion | bytes 49152 | tf_op jit(solution)/shard_map/gather | solution.py:38
  52.9 23.0 %gather_fusion.2 = f32[4096]{0:T(1024)S(1)} fusion(f32[40960]{0:T(1024)S(1)} %copy-done, s32[4096]{0:T(1024)S(1)} %broadcast_clamp_fusion), kind=kCustom, calls=%fused_computation.2 | custom fusion | bytes 49152 | tf_op jit(solution)/shard_map/gather | solution.py:37
  76.0 0.5 convolution_bitcast_fusion.3
  76.5 3.2 fusion.1
  79.7 0.4 fusion.3
  80.2 15.3 %psum.77 = bf16[256,32]{0,1:T(8,128)(2,1)S(1)} all-reduce(bf16[256,32]{0,1:T(8,128)(2,1)S(1)} %fusion.3), channel_id=1, replica_groups=mesh['samp'=64,'var'=4] {'var'}, use_global_device_ids=true, to_apply=%region_0.1 | all-reduce | flops 8192 | bytes 32768 | tf_op jit(solution)/shard_map/psum | solution.py:51
  95.7 1.5 convolution_subtract_fusion.2
  97.3 49.8 %all-reduce.8.cloned.1.call-done = f32[4096,32]{0,1:T(8,128)} async-done(((f32[4096,32]{0,1:T(8,128)}), f32[4096,32]{0,1:T(8,128)}) %all-reduce.8.cloned.1.call-update) | async-done | bytes 524304 | tf_op jit(solution)/shard_map/psum | solution.py:78
  147.4 127.0 %psum.79 = f32[32]{0:T(128)S(1)} all-reduce(f32[32]{0:T(128)S(1)} %get-tuple-element.2), channel_id=1, replica_groups=mesh['samp'=64,'var'=4] {'samp'}, use_global_device_ids=true, to_apply=%region_4.5 | all-reduce | flops 32 | bytes 256 | tf_op jit(solution)/shard_map/psum | solution.py:24
  274.3 0.6 fusion.22
  274.9 60.9 %all-reduce.10.cloned.1.call-done = f32[4096,32]{0,1:T(8,128)} async-done(((f32[4096,32]{0,1:T(8,128)}), f32[4096,32]{0,1:T(8,128)}) %all-reduce.10.cloned.1.call-update) | async-done | bytes 524304 | tf_op jit(solution)/shard_map/psum | solution.py:78
  335.8 1.8 convolution_bitcast_fusion.2
  337.7 1.8 fusion.4
  339.4 14.5 %psum.82 = bf16[256,32]{0,1:T(8,128)(2,1)S(1)} all-reduce(bf16[256,32]{0,1:T(8,128)(2,1)} %fusion.4), channel_id=1, replica_groups=mesh['samp'=64,'var'=4] {'var'}, use_global_device_ids=true, to_apply=%region_8.9 | all-reduce | flops 8192 | bytes 32768 | tf_op jit(solution)/shard_map/psum | solution.py:51
  354.2 1.5 convolution_subtract_fusion.1
  355.8 45.1 %all-reduce.12.cloned.1.call-done = f32[4096,32]{0,1:T(8,128)} async-done(((f32[4096,32]{0,1:T(8,128)}), f32[4096,32]{0,1:T(8,128)}) %all-reduce.12.cloned.1.call-update) | async-done | bytes 524304 | tf_op jit(solution)/shard_map/psum | solution.py:78
  401.0 188.3 %all-reduce.14.cloned.1.call-done = f32[4096,32]{0,1:T(8,128)} async-done(((f32[4096,32]{0,1:T(8,128)}), f32[4096,32]{0,1:T(8,128)}) %all-reduce.14.cloned.1.call-update) | async-done | bytes 524304 | tf_op jit(solution)/shard_map/psum | solution.py:78
  589.3 1.6 multiply_add_fusion
  590.9 0.5 convolution_bitcast_fusion.1
  591.4 0.4 fusion.5
  591.9 13.9 %psum.85 = bf16[256,32]{0,1:T(8,128)(2,1)S(1)} all-reduce(bf16[256,32]{0,1:T(8,128)(2,1)S(1)} %fusion.5), channel_id=1, replica_groups=mesh['samp'=64,'var'=4] {'var'}, use_global_device_ids=true, to_apply=%region_12.13 | all-reduce | flops 8192 | bytes 32768 | tf_op jit(solution)/shard_map/psum | solution.py:51
  606.0 1.5 convolution_subtract_fusion
  607.6 4.6 fusion
  612.2 40.4 %all-reduce.16.cloned.1.call-done = f32[4096,32]{0,1:T(8,128)} async-done(((f32[4096,32]{0,1:T(8,128)}), f32[4096,32]{0,1:T(8,128)}) %all-reduce.16.cloned.1.call-update) | async-done | bytes 524304 | tf_op jit(solution)/shard_map/psum | solution.py:78
  652.7 194.9 %all-reduce.18.cloned.1.call-done = (f32[10240,32]{0,1:T(8,128)}, f32[4096,32]{0,1:T(8,128)}) async-done(((f32[10240,32]{0,1:T(8,128)}, f32[4096,32]{0,1:T(8,128)}), (f32[10240,32]{0,1:T(8,128)}, f32[4096,32]{0,1:T(8,128)})) %all-reduce.18.cloned.1.call-update) | async-done | bytes 1835024 | tf_op jit(solution)/shard_map/psum | solution.py:61
  847.6 1.1 broadcast_multiply_fusion
  848.7 2.3 fusion.2
  851.0 0.8 minimum_subtract_fusion.1
  (67 shorter events, 1.5 us)
Async XLA Ops:
  7.2 140.0 %all-reduce.8.cloned.1.call-start = ((), (), s32[]{:S(2)}) async-start(), calls=%async_computation | async-start | bytes 1048576 | tf_op jit(solution)/shard_map/psum | solution.py:78
  15.2 7.9 copy-start.17
  26.6 3.2 copy-start.1
  29.8 23.1 %copy-start = (f32[40960]{0:T(1024)S(1)}, f32[40960]{0:T(1024)}, u32[]{:S(2)}) copy-start(f32[40960]{0:T(1024)} %param.10) | copy-start | bytes 491524
  52.8 23.1 %copy-start.2 = (f32[4096,32]{0,1:T(8,128)S(1)}, f32[4096,32]{0,1:T(8,128)}, u32[]{:S(2)}) copy-start(f32[4096,32]{0,1:T(8,128)} %param.15) | copy-start | bytes 1572868
  79.7 15.8 %copy-start.4 = (s32[256]{0:T(256)S(1)}, s32[256]{0:T(256)}, u32[]{:S(2)}) copy-start(s32[256]{0:T(256)} %param.13) | copy-start | bytes 3076
  79.7 15.8 %copy-start.5 = (f32[256]{0:T(256)S(1)}, f32[256]{0:T(256)}, u32[]{:S(2)}) copy-start(f32[256]{0:T(256)} %param.12) | copy-start | bytes 3076
  80.1 67.1 %copy-start.16 = (f32[8]{0:T(128)S(1)}, f32[8]{0:T(128)}, u32[]{:S(2)}) copy-start(f32[8]{0:T(128)} %param.16) | copy-start | bytes 100
  80.2 194.2 %copy-start.6 = (f32[32]{0:T(128)S(1)}, f32[32]{0:T(128)}, u32[]{:S(2)}) copy-start(f32[32]{0:T(128)} %param.17) | copy-start | bytes 388
  95.7 51.5 %copy-start.14 = (f32[32]{0:T(128)}, f32[32]{0:T(128)S(1)}, u32[]{:S(2)}) copy-start(f32[32]{0:T(128)S(1)} %get-tuple-element.3) | copy-start | bytes 388
  97.2 238.6 %all-reduce.10.cloned.1.call-start = ((), (), s32[]{:S(2)}) async-start(), calls=%async_computation.1 | async-start | bytes 1048576 | tf_op jit(solution)/shard_map/psum | solution.py:78
  147.1 253.8 %all-reduce.12.cloned.1.call-start = ((), (), s32[]{:S(2)}) async-start(), calls=%async_computation.2 | async-start | bytes 1048576 | tf_op jit(solution)/shard_map/psum | solution.py:78
  147.4 127.6 %copy-start.12 = (f32[32]{0:T(128)}, f32[32]{0:T(128)S(1)}, u32[]{:S(2)}) copy-start(f32[32]{0:T(128)S(1)} %div.40) | copy-start | bytes 388
  335.8 1.8 copy-start.3
  335.8 1.8 copy-start.8
  335.8 1.8 copy-start.10
  355.7 233.5 %all-reduce.14.cloned.1.call-start = ((), (), s32[]{:S(2)}) async-start(), calls=%async_computation.3 | async-start | bytes 1048576 | tf_op jit(solution)/shard_map/psum | solution.py:78
  400.9 251.7 %all-reduce.16.cloned.1.call-start = ((), (), s32[]{:S(2)}) async-start(), calls=%async_computation.4 | async-start | bytes 1048576 | tf_op jit(solution)/shard_map/psum | solution.py:78
  591.9 15.7 %copy-start.15 = (f32[32]{0:T(128)S(1)}, f32[32]{0:T(128)}, u32[]{:S(2)}) copy-start(f32[32]{0:T(128)} %copy-done.14) | copy-start | bytes 388
  607.5 240.1 %all-reduce.18.cloned.1.call-start = ((), (), s32[]{:S(2)}) async-start(), calls=%async_computation.5 | async-start | bytes 3670016 | tf_op jit(solution)/shard_map/psum | solution.py:61
  612.2 236.5 %dynamic-slice-start = ((f32[40960]{0:T(1024)}, s32[]{:T(128)}), f32[10240]{0:T(1024)S(1)}, s32[]{:S(2)}) async-start(f32[40960]{0:T(1024)} %param.11, s32[]{:T(128)} %select_n.39), calls=%async_computation.6 | async-start | bytes 82432 | tf_op jit(solution)/shard_map/dynamic_slice | solution.py:57
  612.2 236.5 %copy-start.13 = (f32[32]{0:T(128)S(1)}, f32[32]{0:T(128)}, u32[]{:S(2)}) copy-start(f32[32]{0:T(128)} %copy-done.12) | copy-start | bytes 388
  652.6 198.3 %copy-start.7 = (f32[32]{0:T(128)S(1)}, f32[32]{0:T(128)}, u32[]{:S(2)}) copy-start(f32[32]{0:T(128)} %param.17) | copy-start | bytes 388
  652.6 198.3 %copy-start.9 = (f32[32]{0:T(128)S(1)}, f32[32]{0:T(128)}, u32[]{:S(2)}) copy-start(f32[32]{0:T(128)} %get-tuple-element.6) | copy-start | bytes 388
  652.7 198.3 %copy-start.11 = (f32[32]{0:T(128)S(1)}, f32[32]{0:T(128)}, u32[]{:S(2)}) copy-start(f32[32]{0:T(128)} %get-tuple-element.7) | copy-start | bytes 388
Sparse Core Ops, SparseCore 0:
  97.3 49.7 all-reduce.7
  150.6 185.1 all-reduce.9
  355.8 45.0 all-reduce.11
  404.2 184.9 all-reduce.13
  607.6 44.9 all-reduce.15
  656.0 191.5 all-reduce.17
